TPU v7x, 32 devices: a whole 2x2x4 slice. The times are simulated.
32 devices in a mesh: gx: 4 (over y, core), gy: 4 (over z), gz: 2 (over x).
Axes of the slice: x: 2, y: 2, z: 4, core: 2. Of those that a mesh axis runs over, the one named last changes fastest.
Arguments:
- orbital_values: bfloat16 [64, 64, 48, 384], P('gx', 'gy', 'gz'), may hold values from -6 to 6
- dm_slabs: bfloat16 [1536, 8, 384], P(('gx', 'gy', 'gz')), may hold values from -0.015625 to 0.015625
- slab_tile: int32 [1536], P(('gx', 'gy', 'gz')), may hold values from 0 to 15, as said below
- slab_place: int32 [1536], P(('gx', 'gy', 'gz')), may hold values from 0 to 47, as said below
Outputs:
- potential: float32 [64, 64, 48], P('gx', 'gy', 'gz')
- pot_slabs: bfloat16 [1536, 8, 384], P(('gx', 'gy', 'gz'))
Inputs may be any that keep to these rules, and one draw needn't show every extreme that they name: `slab_tile`: within each layer along gz, every tile of that layer has exactly one slab for each place 0 .. 47, held by devices of the same layer; no device holds more than 6 slabs of one tile, and in every layer some device holds exactly 6 slabs of some tile. See slab_tile: the pair (slab_tile, slab_place) is different for all slabs of one layer.
All inputs are finite; a program needn't handle non-finite values.
Results may differ from a plain program's by a relative error of at most 0.0023.
Values may be sent and summed in bfloat16 or wider, within the bound.
No kernel may reach another device: no remote copies, remote signals or barrier semaphores. Data moves between devices by JAX's collectives and lax.ppermute only.
A program may use at most 64 MiB of HBM per device.

v0:
```python
import functools
import math

import jax
import jax.numpy as jnp
import numpy as np
from jax import lax
from jax.experimental import pallas as pl
from jax.experimental.pallas import tpu as pltpu
from jax.sharding import PartitionSpec as P


RADIUS = 8
LANES = 128

ALPHAS = (0.012, 0.025, 0.05, 0.1, 0.2, 0.4, 0.8, 1.6)
MIXES = (0.3, 0.3, 0.32, 0.34, 0.36, 0.38, 0.4, 0.42)

VMEM_SPEC = pl.BlockSpec(memory_space=pltpu.VMEM)
SMEM_SPEC = pl.BlockSpec(memory_space=pltpu.SMEM)
HBM_SPEC = pl.BlockSpec(memory_space=pltpu.HBM)


def in_hbm(array):
    return pltpu.with_memory_space_constraint(array, pltpu.HBM)


def grant(mebibytes):
    return pltpu.CompilerParams(vmem_limit_bytes=mebibytes << 20)


def kernel_tables(radius):
    tap_table = [
        [math.exp(-alpha * offset * offset) for offset in range(-radius, radius + 1)]
        for alpha in ALPHAS
    ]
    mix = [
        MIXES[term] / sum((tap * tap for tap in tap_table[term])) ** 1.5
        for term in range(len(ALPHAS))
    ]
    return (tap_table, mix)


def cost(flops, moved_bytes):
    return pl.CostEstimate(flops=flops, bytes_accessed=moved_bytes, transcendentals=0)


def for_each_slab(tile_ref, count_ref, tile_count, slab_count, visit):
    for t in range(tile_count):
        count_ref[t] = 0

    def step(i, carry):
        t = tile_ref[i]
        slot = count_ref[t]
        count_ref[t] = slot + 1
        visit(i, t, slot)
        return carry

    lax.fori_loop(0, slab_count, step, 0, unroll=4)


def pack_kernel(
    capacity, chunks, empty, tile_hbm, place_hbm, slab_hbm, out_ref,
    tile_ref, place_ref, slab_ref, count_ref, label_ref, sems,
):
    copies = [
        pltpu.make_async_copy(tile_hbm, tile_ref, sems.at[0]),
        pltpu.make_async_copy(place_hbm, place_ref, sems.at[1]),
        pltpu.make_async_copy(slab_hbm, slab_ref, sems.at[2]),
    ]
    for copy in copies:
        copy.start()
    tile_count = out_ref.shape[0]
    label_ref[...] = jnp.full(label_ref.shape, empty, jnp.float32)
    out_ref[...] = jnp.zeros(out_ref.shape, out_ref.dtype)
    for copy in copies:
        copy.wait()

    def visit(i, t, slot):
        slab = slab_ref[i]
        for c in range(chunks):
            out_ref[t, slot * chunks + c] = slab[:, c * LANES : (c + 1) * LANES]
        label = place_ref[i].astype(jnp.float32)
        label_ref[t, pl.ds(slot, 1), :] = jnp.full((1, LANES), label, jnp.float32)

    for_each_slab(tile_ref, count_ref, tile_count, slab_ref.shape[0], visit)
    out_ref[:, capacity * chunks] = label_ref[...].astype(jnp.bfloat16)


def odd_row():
    return lax.rem(lax.axis_index("gy"), 2)


def turn_kernel(planes, values_hbm, near_ref, far_hbm, values_ref, far_ref, sems, out_sem):
    points = values_ref.shape[0]
    plane = points // planes
    half = plane // 2
    copies = []
    for x in range(0, planes, 2):
        part = slice(x * plane, (x + 2) * plane)
        copies.append(
            pltpu.make_async_copy(values_hbm.at[part], values_ref.at[part], sems.at[x // 2])
        )
        copies[-1].start()
    near_start = odd_row() * half
    for x in range(0, planes, 2):
        copies[x // 2].wait()
        for start, out_ref in ((near_start, near_ref), (half - near_start, far_ref)):
            rows = [
                values_ref[pl.ds(pl.multiple_of((x + i) * plane + start, half), half), :]
                for i in range(2)
            ]
            out_ref[:, x * half : (x + 2) * half] = jnp.concatenate(rows, axis=0).T
    copy = pltpu.make_async_copy(far_ref, far_hbm, out_sem.at[0])
    copy.start()
    copy.wait()


def arrange(capacity, chunks, arrived_ref, place_ref, wide_ref, turned_ref):
    tile_count, _, rows, _ = arrived_ref.shape
    slots = tile_count * capacity
    labels = arrived_ref[:, capacity * chunks].astype(jnp.float32)[:, :capacity]
    labels = labels.reshape(slots, LANES)
    width = place_ref.shape[1]
    for g in range(width // LANES):
        group = labels[g * LANES : (g + 1) * LANES]
        here = lax.broadcasted_iota(jnp.int32, group.shape, 0) == lax.broadcasted_iota(
            jnp.int32, group.shape, 1
        )
        place_ref[:, g * LANES : (g + 1) * LANES] = jnp.sum(
            jnp.where(here, group, 0.0), axis=0, keepdims=True
        ).astype(jnp.int32)
    first_row = jnp.broadcast_to(labels.reshape(slots, 1, LANES) * rows, (slots, rows, LANES))
    source = first_row + lax.broadcasted_iota(jnp.int32, (slots, rows, LANES), 1).astype(
        jnp.float32
    )
    lane = lax.broadcasted_iota(jnp.int32, (slots, rows, LANES), 2).astype(jnp.float32)
    hot = []
    for c in range(chunks):
        match = jnp.where(source == lane + float(c * LANES), 1.0, 0.0)
        hot.append(match.reshape(slots * rows, LANES).astype(jnp.bfloat16))
    hot = jnp.concatenate(hot, axis=1)
    for c in range(chunks):
        for t in range(tile_count):
            for k in range(capacity):
                row = (t * capacity + k) * rows
                wide_ref[row : row + rows, :] = arrived_ref[t, k * chunks + c].astype(jnp.float32)
        across = wide_ref[...].T.astype(jnp.bfloat16)
        turned_ref[c * LANES : (c + 1) * LANES, :] = jnp.dot(
            across, hot, preferred_element_type=jnp.float32
        ).astype(jnp.bfloat16)


def half_density(piece, turned_ref, values_ref, out_ref):
    half = out_ref.shape[1]
    for q in range(values_ref.shape[1] // piece):
        block = values_ref[:, q * piece : (q + 1) * piece]
        mixed = jnp.dot(turned_ref[...], block, preferred_element_type=jnp.float32)
        density = jnp.sum(mixed * block.astype(jnp.float32), axis=0, keepdims=True)
        for p in range(piece // half):
            row = q * (piece // half) + p
            out_ref[row : row + 1, :] = density[:, p * half : (p + 1) * half]


def near_kernel(
    capacity, chunks, piece, arrived_ref, near_ref, far_hbm,
    out_ref, place_ref, turned_ref, far_ref, wide_ref, sem,
):
    copy = pltpu.make_async_copy(far_hbm, far_ref, sem.at[0])
    copy.start()
    arrange(capacity, chunks, arrived_ref, place_ref, wide_ref, turned_ref)
    half_density(piece, turned_ref, near_ref, out_ref)
    copy.wait()


def far_kernel(piece, turned_ref, far_ref, out_ref):
    half_density(piece, turned_ref, far_ref, out_ref)


def join_kernel(near_ref, far_ref, from_wrap_ref, from_pair_ref, out_ref):
    half = near_ref.shape[1]
    odd = odd_row() == 1
    before = jnp.where(odd, from_pair_ref[...], from_wrap_ref[...])
    low = jnp.where(odd, far_ref[...], near_ref[...])
    high = jnp.where(odd, near_ref[...], far_ref[...])
    after = jnp.where(odd, from_wrap_ref[...], from_pair_ref[...])
    for i, block in enumerate((before, low, high, after)):
        out_ref[:, i * half : (i + 1) * half] = block


def edge_kernel(*refs):
    *block_refs, top_ref, bottom_ref = refs
    rows = top_ref.shape[1]
    for i, ref in enumerate(block_refs):
        top_ref[i] = ref[:rows, :]
        bottom_ref[i] = ref[ref.shape[0] - rows :, :]


def split_dot(left, high, low):
    left_high = left.astype(jnp.bfloat16)
    left_low = (left - left_high.astype(jnp.float32)).astype(jnp.bfloat16)
    out = jnp.dot(left_high, high, preferred_element_type=jnp.float32)
    out = out + jnp.dot(left_low, high, preferred_element_type=jnp.float32)
    return out + jnp.dot(left_high, low, preferred_element_type=jnp.float32)


def filter_kernel(parts, *refs):
    taps_ref, band_high, band_low, fold_high, fold_low, before_ref, after_ref = refs[:7]
    own_refs = refs[7 : 7 + parts]
    out_ref, field_ref, grid_ref, first_ref, second_ref, third_ref = refs[7 + parts :]
    size_x, size_y, size_z = out_ref.shape
    wide_y, wide_x, lanes = first_ref.shape
    for part in range(parts):
        start = 0
        for block in (before_ref.at[part], own_refs[part], after_ref.at[part]):
            rows = block.shape[0]
            for y in range(wide_y):
                grid_ref[y, start : start + rows, part * size_z : (part + 1) * size_z] = block[
                    :, y * size_z : (y + 1) * size_z
                ]
            start += rows
    grid = grid_ref[...].reshape(wide_y * wide_x, parts * size_z)
    first_ref[...] = split_dot(grid, band_high[...], band_low[...]).reshape(wide_y, wide_x, lanes)

    def tap(distance, rows):
        return jnp.broadcast_to(taps_ref[distance : distance + 1, :], (rows, lanes))

    def smooth(y, carry):
        run = tap(0, wide_x) * first_ref[y + RADIUS]
        for d in range(1, RADIUS + 1):
            pair = first_ref[y + (RADIUS - d)] + first_ref[y + (RADIUS + d)]
            run = run + tap(d, wide_x) * pair
        second_ref[y] = run
        run = tap(0, size_x) * second_ref[y, RADIUS : RADIUS + size_x, :]
        for d in range(1, RADIUS + 1):
            pair = (
                second_ref[y, RADIUS - d : RADIUS - d + size_x, :]
                + second_ref[y, RADIUS + d : RADIUS + d + size_x, :]
            )
            run = run + tap(d, size_x) * pair
        third_ref[y] = run
        return carry

    lax.fori_loop(0, size_y, smooth, 0, unroll=4)
    filtered = third_ref[...].reshape(size_y * size_x, lanes)
    folded = split_dot(filtered, fold_high[...], fold_low[...]).reshape(size_y, size_x, size_z)
    for y in range(size_y):
        out_ref[:, y, :] = folded[y]
        field_ref[:, y * size_z : (y + 1) * size_z] = folded[y]


def potential_kernel(
    capacity, chunks, rows, weight, piece, place_vmem, grid_ref, field_ref, near_ref, far_ref,
    out_ref, grid_hbm, total_ref, place_ref, sems,
):
    copies = [
        pltpu.make_async_copy(place_vmem, place_ref, sems.at[0]),
        pltpu.make_async_copy(grid_ref, grid_hbm, sems.at[1]),
    ]
    for copy in copies:
        copy.start()
    list_orb, points = near_ref.shape
    half = field_ref.shape[1] // 2
    odd = odd_row() == 1
    low, high = field_ref[:, :half] * weight, field_ref[:, half:] * weight
    first = True
    for values_ref, source in (
        (near_ref, jnp.where(odd, high, low)),
        (far_ref, jnp.where(odd, low, high)),
    ):
        for q in range(points // piece):
            field = jnp.concatenate(
                [
                    source[x : x + 1, :]
                    for x in range(q * piece // half, (q + 1) * piece // half)
                ],
                axis=1,
            )
            block = values_ref[:, q * piece : (q + 1) * piece]
            weighted = (field * block.astype(jnp.float32)).astype(jnp.bfloat16)
            term = lax.dot_general(
                block, weighted, (((1,), (1,)), ((), ())), preferred_element_type=jnp.float32
            )
            total_ref[...] = term if first else total_ref[...] + term
            first = False

    for copy in copies:
        copy.wait()
    last = list_orb // rows - 1

    def visit(j, carry):
        t, k = j // capacity, j % capacity
        row = pl.multiple_of(jnp.minimum(place_ref[0, j], last) * rows, rows)
        for c in range(chunks):
            lanes = slice(c * LANES, (c + 1) * LANES)
            out_ref[t, k, :, lanes] = total_ref[pl.ds(row, rows), lanes].astype(jnp.bfloat16)
        return carry

    lax.fori_loop(0, out_ref.shape[0] * capacity, visit, 0, unroll=4)


def unpack_kernel(tile_count, tile_ref, back_ref, out_hbm, count_ref, sem):
    def visit(i, t, slot):
        pltpu.make_async_copy(back_ref.at[t, slot], out_hbm.at[i], sem.at[0]).start()

    for_each_slab(tile_ref, count_ref, tile_count, out_hbm.shape[0], visit)
    pltpu.make_async_copy(out_hbm, out_hbm, sem.at[0]).wait()


def moved(block, shifts):
    axes = tuple(shifts)
    sizes = [lax.axis_size(axis) for axis in axes]
    pairs = []
    for source in np.ndindex(*sizes):
        target = [(s + shifts[axis]) % n for s, axis, n in zip(source, axes, sizes)]
        pairs.append(
            (int(np.ravel_multi_index(source, sizes)), int(np.ravel_multi_index(target, sizes)))
        )
    return lax.ppermute(block, axes, pairs)


def band_tables(size_z, neighbours):
    tap_table, mix = kernel_tables(RADIUS)

    def band(shift):
        table = np.zeros((size_z, len(ALPHAS), size_z), np.float64)
        for m in range(len(ALPHAS)):
            for source in range(size_z):
                for target in range(size_z):
                    offset = source + shift - target
                    if abs(offset) <= RADIUS:
                        table[source, m, target] = tap_table[m][offset + RADIUS]
        return table.reshape(size_z, len(ALPHAS) * size_z)

    own, low, high = band(0), band(-size_z), band(size_z)
    bands = {0: [own + low + high], 1: [own, low + high], 2: [own, low, high]}[neighbours]
    taps = np.zeros((16, len(ALPHAS) * size_z), np.float64)
    for d in range(RADIUS + 1):
        taps[d] = np.repeat([row[RADIUS + d] for row in tap_table], size_z)
    fold = np.concatenate([mix[m] * np.eye(size_z) for m in range(len(ALPHAS))], axis=0)

    def split(table):
        high = table.astype(np.float32).astype(jnp.bfloat16)
        low = (table - high.astype(np.float64)).astype(np.float32).astype(jnp.bfloat16)
        return [high, low]

    return [taps.astype(np.float32), *split(np.concatenate(bands, axis=0)), *split(fold)]


def local(orbital_values, dm_slabs, slab_tile, slab_place):
    size_x, size_y, size_z, list_orb = orbital_values.shape
    slab_count, atom_orb, _ = dm_slabs.shape
    list_blk = list_orb // atom_orb
    tile_count = lax.axis_size("gx") * lax.axis_size("gy")
    capacity = max(2, 2 * ((list_blk + tile_count - 1) // tile_count))
    chunks = list_orb // LANES
    tile_points = size_x * size_y * size_z
    plane = size_y * size_z
    counts = pltpu.SMEM((tile_count,), jnp.int32)

    packed = pl.pallas_call(
        functools.partial(pack_kernel, capacity, chunks, float(list_blk)),
        out_shape=jax.ShapeDtypeStruct(
            (tile_count, capacity * chunks + 1, atom_orb, LANES), jnp.bfloat16
        ),
        in_specs=[HBM_SPEC] * 3,
        out_specs=VMEM_SPEC,
        scratch_shapes=[
            pltpu.SMEM((slab_count,), jnp.int32),
            pltpu.SMEM((slab_count,), jnp.int32),
            pltpu.VMEM(dm_slabs.shape, dm_slabs.dtype),
            counts,
            pltpu.VMEM((tile_count, atom_orb, LANES), jnp.float32),
            pltpu.SemaphoreType.DMA((3,)),
        ],
        compiler_params=grant(4),
        name="pack",
    )(in_hbm(slab_tile), in_hbm(slab_place), in_hbm(dm_slabs))
    arrived = lax.all_to_all(packed, ("gx", "gy"), split_axis=0, concat_axis=0, tiled=True)
    half = plane // 2
    half_points = tile_points // 2
    piece = 4 * half
    bf16 = lambda *shape: jax.ShapeDtypeStruct(shape, jnp.bfloat16)
    f32 = lambda *shape: jax.ShapeDtypeStruct(shape, jnp.float32)
    near, far = pl.pallas_call(
        functools.partial(turn_kernel, size_x),
        out_shape=(
            pltpu.VMEM((list_orb, half_points), jnp.bfloat16),
            bf16(list_orb, half_points),
        ),
        in_specs=[HBM_SPEC],
        out_specs=(VMEM_SPEC, HBM_SPEC),
        scratch_shapes=[
            pltpu.VMEM((tile_points, list_orb), jnp.bfloat16),
            pltpu.VMEM((list_orb, half_points), jnp.bfloat16),
            pltpu.SemaphoreType.DMA((size_x // 2,)),
            pltpu.SemaphoreType.DMA((1,)),
        ],
        compiler_params=grant(20),
        cost_estimate=cost(0, 4 * tile_points * list_orb),
        name="turn",
    )(in_hbm(orbital_values.reshape(tile_points, list_orb)))

    slots = LANES * ((tile_count * capacity + LANES - 1) // LANES)
    product = 2 * half_points * list_orb * list_orb
    near_y, places, matrix, far = pl.pallas_call(
        functools.partial(near_kernel, capacity, chunks, piece),
        out_shape=(
            f32(size_x, half),
            jax.ShapeDtypeStruct((1, slots), jnp.int32),
            bf16(list_orb, list_orb),
            pltpu.VMEM((list_orb, half_points), jnp.bfloat16),
        ),
        in_specs=[VMEM_SPEC, VMEM_SPEC, HBM_SPEC],
        out_specs=(VMEM_SPEC,) * 4,
        scratch_shapes=[
            pltpu.VMEM((tile_count * capacity * atom_orb, LANES), jnp.float32),
            pltpu.SemaphoreType.DMA((1,)),
        ],
        compiler_params=grant(20),
        cost_estimate=cost(product, 2 * half_points * list_orb),
        name="near",
    )(arrived, near, in_hbm(far))
    rows = lax.axis_size("gy")
    pair = [(i, i ^ 1) for i in range(rows)]
    wrap = [(i, (i - 1 + 2 * (i % 2)) % rows) for i in range(rows)]
    from_wrap = lax.ppermute(near_y, "gy", wrap)
    far_y = pl.pallas_call(
        functools.partial(far_kernel, piece),
        out_shape=f32(size_x, half),
        in_specs=[VMEM_SPEC, VMEM_SPEC],
        out_specs=VMEM_SPEC,
        compiler_params=grant(20),
        cost_estimate=cost(product, 2 * half_points * list_orb),
        name="far",
    )(matrix, far)
    from_pair = lax.ppermute(far_y, "gy", pair)

    grid = pl.pallas_call(
        join_kernel,
        out_shape=f32(size_x, 2 * plane),
        in_specs=[VMEM_SPEC] * 4,
        out_specs=VMEM_SPEC,
        compiler_params=grant(2),
        name="join",
    )(near_y, far_y, from_wrap, from_pair)
    layers = lax.axis_size("gz")
    blocks = [grid]
    for shift in {1: [], 2: [1]}.get(layers, [1, -1]):
        blocks.append(moved(grid, {"gz": shift}))
    parts = len(blocks)
    top, bottom = pl.pallas_call(
        edge_kernel,
        out_shape=(f32(parts, RADIUS, 2 * plane),) * 2,
        in_specs=[VMEM_SPEC] * parts,
        out_specs=(VMEM_SPEC,) * 2,
        compiler_params=grant(2),
        name="edge",
    )(*blocks)
    before, after = moved(bottom, {"gx": 1}), moved(top, {"gx": -1})
    tables = band_tables(size_z, parts - 1)
    lanes = tables[0].shape[1]
    wide_x, wide_y = size_x + 2 * RADIUS, size_y + 2 * RADIUS
    potential, field = pl.pallas_call(
        functools.partial(filter_kernel, parts),
        out_shape=(pltpu.VMEM((size_x, size_y, size_z), jnp.float32), f32(size_x, plane)),
        in_specs=[VMEM_SPEC] * (len(tables) + 2 + parts),
        out_specs=(VMEM_SPEC,) * 2,
        scratch_shapes=[
            pltpu.VMEM((wide_y, wide_x, parts * size_z), jnp.float32),
            pltpu.VMEM((wide_y, wide_x, lanes), jnp.float32),
            pltpu.VMEM((size_y, wide_x, lanes), jnp.float32),
            pltpu.VMEM((size_y, size_x, lanes), jnp.float32),
        ],
        compiler_params=grant(12),
        name="filter",
    )(*map(jnp.asarray, tables), before, after, *blocks)

    returned, potential = pl.pallas_call(
        functools.partial(
            potential_kernel, capacity, chunks, atom_orb, float(tile_points) ** (-0.5), 2 * piece
        ),
        out_shape=(
            bf16(tile_count, capacity, atom_orb, list_orb),
            f32(size_x, size_y, size_z),
        ),
        in_specs=[VMEM_SPEC] * 5,
        out_specs=(VMEM_SPEC, HBM_SPEC),
        scratch_shapes=[
            pltpu.VMEM((list_orb, list_orb), jnp.float32),
            pltpu.SMEM((1, slots), jnp.int32),
            pltpu.SemaphoreType.DMA((2,)),
        ],
        compiler_params=grant(20),
        name="potential",
    )(places, potential, field, near, far)
    back = lax.all_to_all(returned, ("gx", "gy"), split_axis=0, concat_axis=0, tiled=True)
    own_rows = pl.pallas_call(
        functools.partial(unpack_kernel, tile_count),
        out_shape=bf16(slab_count, atom_orb, list_orb),
        in_specs=[SMEM_SPEC, VMEM_SPEC],
        out_specs=HBM_SPEC,
        scratch_shapes=[counts, pltpu.SemaphoreType.DMA((1,))],
        compiler_params=grant(4),
        name="unpack",
    )(slab_tile, back)
    return (potential, own_rows)


def solution(mesh):
    placed = (
        P("gx", "gy", "gz", None),
        P(("gx", "gy", "gz"), None, None),
        P(("gx", "gy", "gz")),
        P(("gx", "gy", "gz")),
    )

    return jax.shard_map(
        local,
        mesh=mesh,
        in_specs=placed,
        out_specs=(P("gx", "gy", "gz"), P(("gx", "gy", "gz"), None, None)),
        check_vma=False,
    )
```

profile of v0, /device:TPU:0, one launch (start us, length us, event | category | flops | bytes accessed | tf_op | source)
XLA Modules:
  0.0 73.1 jit_solution(13354159850042507217)
XLA Ops:
  0.6 2.1 %pack.1 = bf16[16,19,8,128]{3,2,1,0:T(8,128)(2,1)} custom-call(s32[48]{0:T(128)} %tile_ref.1, s32[48]{0:T(128)} %place_hbm.1, bf16[48,8,384]{2,1,0:T(8,128)(2,1)} %slab_hbm.1), custom_call_target="tpu_custom_call" | custom-call | tf_op jit(solution)/shard_map/pack/pallas_call | solution.py:361
  2.8 7.4 %all-to-all-start = ((bf16[16,19,8,128]{3,2,1,0:T(8,128)(2,1)}), bf16[16,19,8,128]{3,2,1,0:T(8,128)(2,1)S(1)}, u32[]{:S(2)}, u32[]{:S(2)}) async-start(bf16[16,19,8,128]{3,2,1,0:T(8,128)(2,1)} %pack.1), calls=%async_computation | async-start | bytes 1245184 | tf_op jit(solution)/shard_map/all_to_all | solution.py:379
  10.2 3.1 %turn.1 = (bf16[384,3072]{1,0:T(8,128)(2,1)S(1)}, bf16[384,3072]{1,0:T(8,128)(2,1)S(1)}) custom-call(bf16[6144,384]{1,0:T(8,128)(2,1)} %bitcast.1), custom_call_target="tpu_custom_call" | custom-call | bytes 9437184 | tf_op jit(solution)/shard_map/turn/pallas_call | solution.py:385
  13.3 0.0 copy-start
  13.3 1.4 %copy-done = bf16[384,3072]{1,0:T(8,128)(2,1)} copy-done((bf16[384,3072]{1,0:T(8,128)(2,1)}, bf16[384,3072]{1,0:T(8,128)(2,1)S(1)}, u32[]{:S(2)}) %copy-start) | copy-done | bytes 2359320
  14.7 13.2 %all-to-all-done.arrived_ref = bf16[16,19,8,128]{3,2,1,0:T(8,128)(2,1)S(1)} async-done(((bf16[16,19,8,128]{3,2,1,0:T(8,128)(2,1)}), bf16[16,19,8,128]{3,2,1,0:T(8,128)(2,1)S(1)}, u32[]{:S(2)}, u32[]{:S(2)}) %all-to-all-start) | async-done | bytes 622624 | tf_op jit(solution)/shard_map/all_to_all | solution.py:379
  27.9 2.0 %near.1 = (f32[16,192]{1,0:T(8,128)S(1)}, s32[1,128]{1,0:T(1,128)S(1)}, bf16[384,384]{1,0:T(8,128)(2,1)S(1)}, bf16[384,3072]{1,0:T(8,128)(2,1)S(1)}) custom-call(bf16[16,19,8,128]{3,2,1,0:T(8,128)(2,1)S(1)} %all-to-all-done.arrived_ref, bf16[384,3072]{1,0:T(8,128)(2,1)S(1)} %get-tuple-element.14.near_ref, bf16[384,3072]{1,0:T(8,128)(2,1)} %copy-done), custom_call_target="tpu_custom_call" | custom-call | flops 905969664 | bytes 2359296 | tf_op jit(solution)/shard_map/near/pallas_call | solution.py:406
  29.8 0.0 copy-start.1
  29.9 0.0 copy-start.2
  29.9 0.0 copy-start.3
  29.9 0.0 copy-start.4
  29.9 0.0 copy-start.5
  29.9 1.5 %far.1.far_ref = f32[16,192]{1,0:T(8,128)S(1)} custom-call(bf16[384,384]{1,0:T(8,128)(2,1)S(1)} %get-tuple-element.18.turned_ref, bf16[384,3072]{1,0:T(8,128)(2,1)S(1)} %get-tuple-element.19.far_ref), custom_call_target="tpu_custom_call" | custom-call | flops 905969664 | bytes 2359296 | tf_op jit(solution)/shard_map/far/pallas_call | solution.py:428
  31.4 0.0 collective-permute-start.1
  31.5 1.1 %collective-permute-start = (f32[16,192]{1,0:T(8,128)S(1)}, f32[16,192]{1,0:T(8,128)S(1)}, u32[]{:S(2)}, u32[]{:S(2)}) collective-permute-start(f32[16,192]{1,0:T(8,128)S(1)} %get-tuple-element.17.near_ref), channel_id=1, source_target_pairs={{0,6},{2,4},{4,2},{6,0},{1,7},{3,5},{5,3},{7,1},{8,14},{10,12},{12... | collective-permute-start | bytes 36872 | tf_op jit(solution)/shard_map/ppermute | solution.py:427
  32.5 2.6 %collective-permute-done.1.from_pair_ref = f32[16,192]{1,0:T(8,128)S(1)} collective-permute-done((f32[16,192]{1,0:T(8,128)S(1)}, f32[16,192]{1,0:T(8,128)S(1)}, u32[]{:S(2)}, u32[]{:S(2)}) %collective-permute-start.1) | collective-permute-done | bytes 12320 | tf_op jit(solution)/shard_map/ppermute | solution.py:437
  35.2 1.9 %collective-permute-done.from_wrap_ref = f32[16,192]{1,0:T(8,128)S(1)} collective-permute-done((f32[16,192]{1,0:T(8,128)S(1)}, f32[16,192]{1,0:T(8,128)S(1)}, u32[]{:S(2)}, u32[]{:S(2)}) %collective-permute-start) | collective-permute-done | bytes 12320 | tf_op jit(solution)/shard_map/ppermute | solution.py:427
  37.1 0.1 join.1.refs_0_.refs_7_
  37.1 1.5 %collective-permute-start.2 = (f32[16,768]{1,0:T(8,128)S(1)}, f32[16,768]{1,0:T(8,128)S(1)}, u32[]{:S(2)}, u32[]{:S(2)}) collective-permute-start(f32[16,768]{1,0:T(8,128)S(1)} %join.1.refs_0_.refs_7_), channel_id=1, source_target_pairs={{0,1},{1,0},{2,3},{3,2},{4,5},{5,4},{6,7},{7,6},{8,9},{9,8},{10,11... | collective-permute-start | bytes 147464 | tf_op jit(solution)/shard_map/ppermute | solution.py:319
  38.6 2.6 %collective-permute-done.2.refs_1_.refs_8_ = f32[16,768]{1,0:T(8,128)S(1)} collective-permute-done((f32[16,768]{1,0:T(8,128)S(1)}, f32[16,768]{1,0:T(8,128)S(1)}, u32[]{:S(2)}, u32[]{:S(2)}) %collective-permute-start.2) | collective-permute-done | bytes 49184 | tf_op jit(solution)/shard_map/ppermute | solution.py:319
  41.2 0.1 collective-permute-start.3
  41.3 1.7 %collective-permute-start.4 = (f32[2,8,768]{2,1,0:T(8,128)S(1)}, f32[2,8,768]{2,1,0:T(8,128)S(1)}, u32[]{:S(2)}, u32[]{:S(2)}) collective-permute-start(f32[2,8,768]{2,1,0:T(8,128)S(1)} %get-tuple-element.21), channel_id=1, source_target_pairs={{0,24},{8,0},{16,8},{24,16},{1,25},{9,1},{17,9},{25,17},{2,26},{10... | collective-permute-start | bytes 147464 | tf_op jit(solution)/shard_map/ppermute | solution.py:319
  43.0 1.8 %collective-permute-done.3.refs_5_ = f32[2,8,768]{2,1,0:T(8,128)S(1)} collective-permute-done((f32[2,8,768]{2,1,0:T(8,128)S(1)}, f32[2,8,768]{2,1,0:T(8,128)S(1)}, u32[]{:S(2)}, u32[]{:S(2)}) %collective-permute-start.3) | collective-permute-done | bytes 49184 | tf_op jit(solution)/shard_map/ppermute | solution.py:319
  44.8 0.0 collective-permute-done.4.refs_6_
  44.8 0.0 copy-done.1
  44.8 0.0 copy-done.2
  44.8 0.0 copy-done.3
  44.8 0.0 copy-done.4
  44.8 0.0 copy-done.5
  44.9 2.2 %filter.1 = (f32[16,16,24]{2,1,0:T(8,128)S(1)}, f32[16,384]{1,0:T(8,128)S(1)}) custom-call(f32[16,192]{1,0:T(8,128)S(1)} %copy-done.5, bf16[48,192]{1,0:T(8,128)(2,1)S(1)} %copy-done.4, bf16[48,192]{1,0:T(8,128)(2,1)S(1)} %copy-done.3, bf16[192,24]{1,0:T(8,128)(2,1)S(1)} %copy-done.2, bf16[192,24]{1,0:T(8,128)(2,1)S(1)} %copy-done.1, ...), custom_call_target="tpu_custom_call" | custom-call | tf_op jit(solution)/shard_map/filter/pallas_call | solution.py:464
  47.1 0.0 copy-start.6
  47.1 3.7 %potential.1 = (bf16[16,6,8,384]{3,2,1,0:T(8,128)(2,1)S(1)}, f32[16,16,24]{2,1,0:T(8,128)}) custom-call(s32[1,128]{1,0:T(1,128)S(1)} %get-tuple-element.16.place_vmem, f32[16,16,24]{2,1,0:T(8,128)S(1)} %get-tuple-element.22.grid_ref, f32[16,384]{1,0:T(8,128)S(1)} %get-tuple-element.23.field_ref, bf16[384,3072]{1,0:T(8,128)(2,1)S(1)} %get-tuple-element.14.near_ref, ...), custom_call_target="tpu_custom_call" | custom-call | tf_op jit(solution)/shard_map/potential/pallas_call | solution.py:479
  50.9 20.8 %all_to_all.10.back_ref = bf16[16,6,8,384]{3,2,1,0:T(8,128)(2,1)S(1)} all-to-all(bf16[16,6,8,384]{3,2,1,0:T(8,128)(2,1)S(1)} %get-tuple-element.25), channel_id=1, replica_groups=mesh['gx'=4,'gy'=4,'gz'=2] {'gx','gy'}, dimensions={0} | all-to-all | bytes 1179648 | tf_op jit(solution)/shard_map/all_to_all | solution.py:497
  71.7 0.0 copy-done.6
  71.7 1.4 %unpack.1 = bf16[48,8,384]{2,1,0:T(8,128)(2,1)} custom-call(s32[48]{0:T(128)S(1)} %copy-done.6, bf16[16,6,8,384]{3,2,1,0:T(8,128)(2,1)S(1)} %all_to_all.10.back_ref), custom_call_target="tpu_custom_call" | custom-call | tf_op jit(solution)/shard_map/unpack/pallas_call | solution.py:498
  (1 shorter events, 0.0 us)
Async XLA Ops:
  2.8 25.1 %all-to-all-start = ((bf16[16,19,8,128]{3,2,1,0:T(8,128)(2,1)}), bf16[16,19,8,128]{3,2,1,0:T(8,128)(2,1)S(1)}, u32[]{:S(2)}, u32[]{:S(2)}) async-start(bf16[16,19,8,128]{3,2,1,0:T(8,128)(2,1)} %pack.1), calls=%async_computation | async-start | bytes 1245184 | tf_op jit(solution)/shard_map/all_to_all | solution.py:379
  13.3 1.4 %copy-start = (bf16[384,3072]{1,0:T(8,128)(2,1)}, bf16[384,3072]{1,0:T(8,128)(2,1)S(1)}, u32[]{:S(2)}) copy-start(bf16[384,3072]{1,0:T(8,128)(2,1)S(1)} %get-tuple-element.15.far_hbm) | copy-start | bytes 7077892
  29.8 15.0 %copy-start.1 = (bf16[192,24]{1,0:T(8,128)(2,1)S(1)}, bf16[192,24]{1,0:T(8,128)(2,1)}, u32[]{:S(2)}) copy-start(bf16[192,24]{1,0:T(8,128)(2,1)} %constant.14.clone.refs_4_) | copy-start | bytes 27652
  29.9 15.0 %copy-start.2 = (bf16[192,24]{1,0:T(8,128)(2,1)S(1)}, bf16[192,24]{1,0:T(8,128)(2,1)}, u32[]{:S(2)}) copy-start(bf16[192,24]{1,0:T(8,128)(2,1)} %constant.13.clone.refs_3_) | copy-start | bytes 27652
  29.9 15.0 %copy-start.3 = (bf16[48,192]{1,0:T(8,128)(2,1)S(1)}, bf16[48,192]{1,0:T(8,128)(2,1)}, u32[]{:S(2)}) copy-start(bf16[48,192]{1,0:T(8,128)(2,1)} %constant.12.clone.refs_2_) | copy-start | bytes 55300
  29.9 14.9 %copy-start.4 = (bf16[48,192]{1,0:T(8,128)(2,1)S(1)}, bf16[48,192]{1,0:T(8,128)(2,1)}, u32[]{:S(2)}) copy-start(bf16[48,192]{1,0:T(8,128)(2,1)} %constant.11.clone.refs_1_) | copy-start | bytes 55300
  29.9 14.9 %copy-start.5 = (f32[16,192]{1,0:T(8,128)S(1)}, f32[16,192]{1,0:T(8,128)}, u32[]{:S(2)}) copy-start(f32[16,192]{1,0:T(8,128)} %constant.10.clone.refs_0_) | copy-start | bytes 36868
  31.4 3.7 %collective-permute-start.1 = (f32[16,192]{1,0:T(8,128)S(1)}, f32[16,192]{1,0:T(8,128)S(1)}, u32[]{:S(2)}, u32[]{:S(2)}) collective-permute-start(f32[16,192]{1,0:T(8,128)S(1)} %far.1.far_ref), channel_id=1, source_target_pairs={{0,2},{2,0},{4,6},{6,4},{1,3},{3,1},{5,7},{7,5},{8,10},{10,8},{12,... | collective-permute-start | bytes 36872 | tf_op jit(solution)/shard_map/ppermute | solution.py:437
  31.5 5.6 %collective-permute-start = (f32[16,192]{1,0:T(8,128)S(1)}, f32[16,192]{1,0:T(8,128)S(1)}, u32[]{:S(2)}, u32[]{:S(2)}) collective-permute-start(f32[16,192]{1,0:T(8,128)S(1)} %get-tuple-element.17.near_ref), channel_id=1, source_target_pairs={{0,6},{2,4},{4,2},{6,0},{1,7},{3,5},{5,3},{7,1},{8,14},{10,12},{12... | collective-permute-start | bytes 36872 | tf_op jit(solution)/shard_map/ppermute | solution.py:427
  37.1 4.1 %collective-permute-start.2 = (f32[16,768]{1,0:T(8,128)S(1)}, f32[16,768]{1,0:T(8,128)S(1)}, u32[]{:S(2)}, u32[]{:S(2)}) collective-permute-start(f32[16,768]{1,0:T(8,128)S(1)} %join.1.refs_0_.refs_7_), channel_id=1, source_target_pairs={{0,1},{1,0},{2,3},{3,2},{4,5},{5,4},{6,7},{7,6},{8,9},{9,8},{10,11... | collective-permute-start | bytes 147464 | tf_op jit(solution)/shard_map/ppermute | solution.py:319
  41.2 3.6 %collective-permute-start.3 = (f32[2,8,768]{2,1,0:T(8,128)S(1)}, f32[2,8,768]{2,1,0:T(8,128)S(1)}, u32[]{:S(2)}, u32[]{:S(2)}) collective-permute-start(f32[2,8,768]{2,1,0:T(8,128)S(1)} %get-tuple-element.20), channel_id=1, source_target_pairs={{0,8},{8,16},{16,24},{24,0},{1,9},{9,17},{17,25},{25,1},{2,10},{10... | collective-permute-start | bytes 147464 | tf_op jit(solution)/shard_map/ppermute | solution.py:319
  41.3 3.5 %collective-permute-start.4 = (f32[2,8,768]{2,1,0:T(8,128)S(1)}, f32[2,8,768]{2,1,0:T(8,128)S(1)}, u32[]{:S(2)}, u32[]{:S(2)}) collective-permute-start(f32[2,8,768]{2,1,0:T(8,128)S(1)} %get-tuple-element.21), channel_id=1, source_target_pairs={{0,24},{8,0},{16,8},{24,16},{1,25},{9,1},{17,9},{25,17},{2,26},{10... | collective-permute-start | bytes 147464 | tf_op jit(solution)/shard_map/ppermute | solution.py:319
  47.1 24.6 %copy-start.6 = (s32[48]{0:T(128)S(1)}, s32[48]{0:T(128)}, u32[]{:S(2)}) copy-start(s32[48]{0:T(128)} %tile_ref.1) | copy-start | bytes 580
where the time goes:
time: 73.4 us; the launch traced here: 73.1 us
  waiting for transfers between devices  22.1 us (30%)
  blocking collectives  20.8 us (28%)
  Pallas kernels  16.2 us (22%)
  starting transfers between devices  11.8 us (16%)
  local copies, waits for them, and re-layouts  1.46 us (2%)
  between operations  0.78 us (1%)
    all_to_all x1, blocking collectives, local(): lax.all_to_all(returned, ('gx', 'gy'), split_axis=0, concat_axis=0, tiled...  20.8 us
    all_to_all x1, waiting for transfers between devices, local(): lax.all_to_all(packed, ('gx', 'gy'), split_axis=0, concat_axis=0, tiled=T...  13.2 us
    all_to_all x1, starting transfers between devices, local(): lax.all_to_all(packed, ('gx', 'gy'), split_axis=0, concat_axis=0, tiled=T...  7.42 us
    ppermute x3, waiting for transfers between devices, moved(): return lax.ppermute(block, axes, pairs)  4.38 us
    pallas_call x1, Pallas kernels, local(): pl.pallas_call(functools.partial(potential_kernel, capacity, chunks, atom...  3.74 us
    ppermute x3, starting transfers between devices, moved(): return lax.ppermute(block, axes, pairs)  3.28 us
    pallas_call x1, Pallas kernels, local(): pl.pallas_call(functools.partial(turn_kernel, size_x), out_shape=(pltpu.V...  3.07 us
    ppermute x1, waiting for transfers between devices, local(): from_pair = lax.ppermute(far_y, 'gy', pair)  2.65 us
  transfers between devices with their start and end apart: 6, of which 5 were waited for; matrix products, arithmetic and copies ran while one was open for 0% of the time, Pallas kernels for 4%

commit v1 on v0

--- a/solution.py
+++ b/solution.py
@@ -177,23 +177,24 @@
     half_density(piece, turned_ref, far_ref, out_ref)
 
 
-def join_kernel(near_ref, far_ref, from_wrap_ref, from_pair_ref, out_ref):
-    half = near_ref.shape[1]
+def join_kernel(*refs):
+    *half_refs, out_ref, top_ref, bottom_ref = refs
+    parts, size_x, _ = out_ref.shape
+    reach = top_ref.shape[1]
+    half = half_refs[0].shape[1]
     odd = odd_row() == 1
-    before = jnp.where(odd, from_pair_ref[...], from_wrap_ref[...])
-    low = jnp.where(odd, far_ref[...], near_ref[...])
-    high = jnp.where(odd, near_ref[...], far_ref[...])
-    after = jnp.where(odd, from_wrap_ref[...], from_pair_ref[...])
-    for i, block in enumerate((before, low, high, after)):
-        out_ref[:, i * half : (i + 1) * half] = block
-
-
-def edge_kernel(*refs):
-    *block_refs, top_ref, bottom_ref = refs
-    rows = top_ref.shape[1]
-    for i, ref in enumerate(block_refs):
-        top_ref[i] = ref[:rows, :]
-        bottom_ref[i] = ref[ref.shape[0] - rows :, :]
+    for part in range(parts):
+        near, far, wrap, pair = (ref[...] for ref in half_refs[4 * part : 4 * part + 4])
+        blocks = (
+            jnp.where(odd, pair, wrap),
+            jnp.where(odd, far, near),
+            jnp.where(odd, near, far),
+            jnp.where(odd, wrap, pair),
+        )
+        for i, block in enumerate(blocks):
+            out_ref[part, :, i * half : (i + 1) * half] = block
+        top_ref[part] = out_ref[part, :reach, :]
+        bottom_ref[part] = out_ref[part, size_x - reach :, :]
 
 
 def split_dot(left, high, low):
@@ -206,13 +207,12 @@
 
 def filter_kernel(parts, *refs):
     taps_ref, band_high, band_low, fold_high, fold_low, before_ref, after_ref = refs[:7]
-    own_refs = refs[7 : 7 + parts]
-    out_ref, field_ref, grid_ref, first_ref, second_ref, third_ref = refs[7 + parts :]
+    own_ref, out_ref, field_ref, grid_ref, first_ref, second_ref, third_ref = refs[7:]
     size_x, size_y, size_z = out_ref.shape
     wide_y, wide_x, lanes = first_ref.shape
     for part in range(parts):
         start = 0
-        for block in (before_ref.at[part], own_refs[part], after_ref.at[part]):
+        for block in (before_ref.at[part], own_ref.at[part], after_ref.at[part]):
             rows = block.shape[0]
             for y in range(wide_y):
                 grid_ref[y, start : start + rows, part * size_z : (part + 1) * size_z] = block[
@@ -307,14 +307,13 @@
     pltpu.make_async_copy(out_hbm, out_hbm, sem.at[0]).wait()
 
 
-def moved(block, shifts):
-    axes = tuple(shifts)
+def moved(block, axes, targets):
     sizes = [lax.axis_size(axis) for axis in axes]
     pairs = []
-    for source in np.ndindex(*sizes):
-        target = [(s + shifts[axis]) % n for s, axis, n in zip(source, axes, sizes)]
+    for place in np.ndindex(*sizes):
+        target = [t % n for t, n in zip(targets(*place), sizes)]
         pairs.append(
-            (int(np.ravel_multi_index(source, sizes)), int(np.ravel_multi_index(target, sizes)))
+            (int(np.ravel_multi_index(place, sizes)), int(np.ravel_multi_index(target, sizes)))
         )
     return lax.ppermute(block, axes, pairs)
 
@@ -421,10 +420,14 @@
         cost_estimate=cost(product, 2 * half_points * list_orb),
         name="near",
     )(arrived, near, in_hbm(far))
-    rows = lax.axis_size("gy")
-    pair = [(i, i ^ 1) for i in range(rows)]
-    wrap = [(i, (i - 1 + 2 * (i % 2)) % rows) for i in range(rows)]
-    from_wrap = lax.ppermute(near_y, "gy", wrap)
+    shifts = {1: [], 2: [1]}.get(lax.axis_size("gz"), [1, -1])
+    wrap = lambda row: row - 1 + 2 * (row % 2)
+    pair = lambda row: row + 1 - 2 * (row % 2)
+    near_wrap = [moved(near_y, ("gy",), lambda row: (wrap(row),))]
+    near_own = [near_y]
+    for shift in shifts:
+        near_own.append(moved(near_y, ("gz",), lambda layer: (layer + shift,)))
+        near_wrap.append(moved(near_y, ("gy", "gz"), lambda row, layer: (wrap(row), layer + shift)))
     far_y = pl.pallas_call(
         functools.partial(far_kernel, piece),
         out_shape=f32(size_x, half),
@@ -434,37 +437,36 @@
         cost_estimate=cost(product, 2 * half_points * list_orb),
         name="far",
     )(matrix, far)
-    from_pair = lax.ppermute(far_y, "gy", pair)
-
-    grid = pl.pallas_call(
+    far_pair = [moved(far_y, ("gy",), lambda row: (pair(row),))]
+    far_own = [far_y]
+    for shift in shifts:
+        far_own.append(moved(far_y, ("gz",), lambda layer: (layer + shift,)))
+        far_pair.append(
+            moved(far_y, ("gy", "gz"), lambda row, layer: (pair(row), layer + shift))
+        )
+    halves = [h for group in zip(near_own, far_own, near_wrap, far_pair) for h in group]
+    parts = 1 + len(shifts)
+    own, top, bottom = pl.pallas_call(
         join_kernel,
-        out_shape=f32(size_x, 2 * plane),
-        in_specs=[VMEM_SPEC] * 4,
-        out_specs=VMEM_SPEC,
+        out_shape=(
+            f32(parts, size_x, 2 * plane),
+            f32(parts, RADIUS, 2 * plane),
+            f32(parts, RADIUS, 2 * plane),
+        ),
+        in_specs=[VMEM_SPEC] * len(halves),
+        out_specs=(VMEM_SPEC,) * 3,
         compiler_params=grant(2),
         name="join",
-    )(near_y, far_y, from_wrap, from_pair)
-    layers = lax.axis_size("gz")
-    blocks = [grid]
-    for shift in {1: [], 2: [1]}.get(layers, [1, -1]):
-        blocks.append(moved(grid, {"gz": shift}))
-    parts = len(blocks)
-    top, bottom = pl.pallas_call(
-        edge_kernel,
-        out_shape=(f32(parts, RADIUS, 2 * plane),) * 2,
-        in_specs=[VMEM_SPEC] * parts,
-        out_specs=(VMEM_SPEC,) * 2,
-        compiler_params=grant(2),
-        name="edge",
-    )(*blocks)
-    before, after = moved(bottom, {"gx": 1}), moved(top, {"gx": -1})
+    )(*halves)
+    before = moved(bottom, ("gx",), lambda column: (column + 1,))
+    after = moved(top, ("gx",), lambda column: (column - 1,))
     tables = band_tables(size_z, parts - 1)
     lanes = tables[0].shape[1]
     wide_x, wide_y = size_x + 2 * RADIUS, size_y + 2 * RADIUS
     potential, field = pl.pallas_call(
         functools.partial(filter_kernel, parts),
         out_shape=(pltpu.VMEM((size_x, size_y, size_z), jnp.float32), f32(size_x, plane)),
-        in_specs=[VMEM_SPEC] * (len(tables) + 2 + parts),
+        in_specs=[VMEM_SPEC] * (len(tables) + 3),
         out_specs=(VMEM_SPEC,) * 2,
         scratch_shapes=[
             pltpu.VMEM((wide_y, wide_x, parts * size_z), jnp.float32),
@@ -474,7 +476,7 @@
         ],
         compiler_params=grant(12),
         name="filter",
-    )(*map(jnp.asarray, tables), before, after, *blocks)
+    )(*map(jnp.asarray, tables), before, after, own)
 
     returned, potential = pl.pallas_call(
         functools.partial(

time: 73.4 us -> 76.8 us (1.046)
  starting transfers between devices: 11.8 us -> 18 us
  waiting for transfers between devices: 22.1 us -> 17.7 us
  blocking collectives: 20.8 us -> 22.4 us
    ppermute x3 -> x8, starting transfers between devices: 3.28 us -> 10.6 us  [moved(): return lax.ppermute(block, axes, pairs)]
    ppermute x2 -> x0, waiting for transfers between devices: 4.52 us -> none  [the longest x1 2.65 us: local(): from_pair = lax.ppermute(far_y, 'gy', pair)]
    all_to_all x1, blocking collectives: 20.8 us -> 22.4 us  [local(): lax.all_to_all(returned, ('gx', 'gy'), split_axis=0, concat_axis=0, tiled...]
    ppermute x2 -> x0, starting transfers between devices: 1.09 us -> none  [the longest x1 1.08 us: local(): from_wrap = lax.ppermute(near_y, 'gy', wrap)]
    ppermute x3 -> x8, waiting for transfers between devices: 4.38 us -> 4.5 us  [moved(): return lax.ppermute(block, axes, pairs)]
  transfers between devices with their start and end apart: 6 -> 9, of which waited for: 5 -> 4; matrix products, arithmetic and copies ran while one was open for 0% -> 0% of each run, Pallas kernels for 4% -> 4%
where the time goes in v1:
time: 76.8 us; the launch traced here: 76.5 us
  blocking collectives  22.4 us (29%)
  starting transfers between devices  18 us (23%)
  waiting for transfers between devices  17.7 us (23%)
  Pallas kernels  16.2 us (21%)
  local copies, waits for them, and re-layouts  1.47 us (2%)
  between operations  0.77 us (1%)
    all_to_all x1, blocking collectives, local(): lax.all_to_all(returned, ('gx', 'gy'), split_axis=0, concat_axis=0, tiled...  22.4 us
    all_to_all x1, waiting for transfers between devices, local(): lax.all_to_all(packed, ('gx', 'gy'), split_axis=0, concat_axis=0, tiled=T...  13.2 us
    ppermute x8, starting transfers between devices, moved(): return lax.ppermute(block, axes, pairs)  10.6 us
    all_to_all x1, starting transfers between devices, local(): lax.all_to_all(packed, ('gx', 'gy'), split_axis=0, concat_axis=0, tiled=T...  7.42 us
    ppermute x8, waiting for transfers between devices, moved(): return lax.ppermute(block, axes, pairs)  4.5 us
    pallas_call x1, Pallas kernels, local(): pl.pallas_call(functools.partial(potential_kernel, capacity, chunks, atom...  3.74 us
    pallas_call x1, Pallas kernels, local(): pl.pallas_call(functools.partial(turn_kernel, size_x), out_shape=(pltpu.V...  3.07 us
    pallas_call x1, Pallas kernels, local(): pl.pallas_call(functools.partial(filter_kernel, parts), out_shape=(pltpu....  2.25 us
  transfers between devices with their start and end apart: 9, of which 4 were waited for; matrix products, arithmetic and copies ran while one was open for 0% of the time, Pallas kernels for 4%

profile of v1, /device:TPU:0, one launch (start us, length us, event | category | flops | bytes accessed | tf_op | source)
XLA Modules:
  0.0 76.5 jit_solution(5237963605918970974)
XLA Ops:
  0.6 2.1 %pack.1 = bf16[16,19,8,128]{3,2,1,0:T(8,128)(2,1)} custom-call(s32[48]{0:T(128)} %tile_ref.1, s32[48]{0:T(128)} %place_hbm.1, bf16[48,8,384]{2,1,0:T(8,128)(2,1)} %slab_hbm.1), custom_call_target="tpu_custom_call" | custom-call | tf_op jit(solution)/shard_map/pack/pallas_call | solution.py:360
  2.8 7.4 %all-to-all-start = ((bf16[16,19,8,128]{3,2,1,0:T(8,128)(2,1)}), bf16[16,19,8,128]{3,2,1,0:T(8,128)(2,1)S(1)}, u32[]{:S(2)}, u32[]{:S(2)}) async-start(bf16[16,19,8,128]{3,2,1,0:T(8,128)(2,1)} %pack.1), calls=%async_computation | async-start | bytes 1245184 | tf_op jit(solution)/shard_map/all_to_all | solution.py:378
  10.2 3.1 %turn.1 = (bf16[384,3072]{1,0:T(8,128)(2,1)S(1)}, bf16[384,3072]{1,0:T(8,128)(2,1)S(1)}) custom-call(bf16[6144,384]{1,0:T(8,128)(2,1)} %bitcast.1), custom_call_target="tpu_custom_call" | custom-call | bytes 9437184 | tf_op jit(solution)/shard_map/turn/pallas_call | solution.py:384
  13.3 0.0 copy-start
  13.3 1.4 %copy-done = bf16[384,3072]{1,0:T(8,128)(2,1)} copy-done((bf16[384,3072]{1,0:T(8,128)(2,1)}, bf16[384,3072]{1,0:T(8,128)(2,1)S(1)}, u32[]{:S(2)}) %copy-start) | copy-done | bytes 2359320
  14.7 13.2 %all-to-all-done.arrived_ref = bf16[16,19,8,128]{3,2,1,0:T(8,128)(2,1)S(1)} async-done(((bf16[16,19,8,128]{3,2,1,0:T(8,128)(2,1)}), bf16[16,19,8,128]{3,2,1,0:T(8,128)(2,1)S(1)}, u32[]{:S(2)}, u32[]{:S(2)}) %all-to-all-start) | async-done | bytes 622624 | tf_op jit(solution)/shard_map/all_to_all | solution.py:378
  27.9 2.0 %near.1 = (f32[16,192]{1,0:T(8,128)S(1)}, s32[1,128]{1,0:T(1,128)S(1)}, bf16[384,384]{1,0:T(8,128)(2,1)S(1)}, bf16[384,3072]{1,0:T(8,128)(2,1)S(1)}) custom-call(bf16[16,19,8,128]{3,2,1,0:T(8,128)(2,1)S(1)} %all-to-all-done.arrived_ref, bf16[384,3072]{1,0:T(8,128)(2,1)S(1)} %get-tuple-element.15.near_ref, bf16[384,3072]{1,0:T(8,128)(2,1)} %copy-done), custom_call_target="tpu_custom_call" | custom-call | flops 905969664 | bytes 2359296 | tf_op jit(solution)/shard_map/near/pallas_call | solution.py:405
  29.8 0.0 copy-start.1
  29.9 0.0 copy-start.2
  29.9 0.0 copy-start.3
  29.9 0.0 copy-start.4
  29.9 0.0 copy-start.5
  29.9 1.5 %far.1.refs_1_ = f32[16,192]{1,0:T(8,128)S(1)} custom-call(bf16[384,384]{1,0:T(8,128)(2,1)S(1)} %get-tuple-element.19.turned_ref, bf16[384,3072]{1,0:T(8,128)(2,1)S(1)} %get-tuple-element.20.far_ref), custom_call_target="tpu_custom_call" | custom-call | flops 905969664 | bytes 2359296 | tf_op jit(solution)/shard_map/far/pallas_call | solution.py:431
  31.4 0.8 collective-permute-start.5
  32.2 0.8 %collective-permute-start.3 = (f32[16,192]{1,0:T(8,128)S(1)}, f32[16,192]{1,0:T(8,128)S(1)}, u32[]{:S(2)}, u32[]{:S(2)}) collective-permute-start(f32[16,192]{1,0:T(8,128)S(1)} %far.1.refs_1_), channel_id=1, source_target_pairs={{0,1},{1,0},{2,3},{3,2},{4,5},{5,4},{6,7},{7,6},{8,9},{9,8},{10,11... | collective-permute-start | bytes 36872 | tf_op jit(solution)/shard_map/ppermute | solution.py:318
  33.0 1.9 %collective-permute-start.1 = (f32[16,192]{1,0:T(8,128)S(1)}, f32[16,192]{1,0:T(8,128)S(1)}, u32[]{:S(2)}, u32[]{:S(2)}) collective-permute-start(f32[16,192]{1,0:T(8,128)S(1)} %far.1.refs_1_), channel_id=1, source_target_pairs={{0,2},{2,0},{4,6},{6,4},{1,3},{3,1},{5,7},{7,5},{8,10},{10,8},{12,... | collective-permute-start | bytes 36872 | tf_op jit(solution)/shard_map/ppermute | solution.py:318
  34.9 1.9 %collective-permute-start.4 = (f32[16,192]{1,0:T(8,128)S(1)}, f32[16,192]{1,0:T(8,128)S(1)}, u32[]{:S(2)}, u32[]{:S(2)}) collective-permute-start(f32[16,192]{1,0:T(8,128)S(1)} %get-tuple-element.18.refs_0_), channel_id=1, source_target_pairs={{0,7},{1,6},{2,5},{3,4},{4,3},{5,2},{6,1},{7,0},{8,15},{9,14},{10,... | collective-permute-start | bytes 36872 | tf_op jit(solution)/shard_map/ppermute | solution.py:318
  36.9 0.5 collective-permute-start.2
  37.4 0.0 collective-permute-done.5.refs_7_
  37.4 2.8 %collective-permute-start = (f32[16,192]{1,0:T(8,128)S(1)}, f32[16,192]{1,0:T(8,128)S(1)}, u32[]{:S(2)}, u32[]{:S(2)}) collective-permute-start(f32[16,192]{1,0:T(8,128)S(1)} %get-tuple-element.18.refs_0_), channel_id=1, source_target_pairs={{0,6},{2,4},{4,2},{6,0},{1,7},{3,5},{5,3},{7,1},{8,14},{10,12},{12... | collective-permute-start | bytes 36872 | tf_op jit(solution)/shard_map/ppermute | solution.py:318
  40.2 0.0 collective-permute-done.3.refs_5_
  40.2 0.0 collective-permute-done.1.refs_3_
  40.2 1.1 %collective-permute-done.4.refs_6_ = f32[16,192]{1,0:T(8,128)S(1)} collective-permute-done((f32[16,192]{1,0:T(8,128)S(1)}, f32[16,192]{1,0:T(8,128)S(1)}, u32[]{:S(2)}, u32[]{:S(2)}) %collective-permute-start.4) | collective-permute-done | bytes 12320 | tf_op jit(solution)/shard_map/ppermute | solution.py:318
  41.4 0.0 collective-permute-done.2.refs_4_
  41.4 1.6 %collective-permute-done.refs_2_ = f32[16,192]{1,0:T(8,128)S(1)} collective-permute-done((f32[16,192]{1,0:T(8,128)S(1)}, f32[16,192]{1,0:T(8,128)S(1)}, u32[]{:S(2)}, u32[]{:S(2)}) %collective-permute-start) | collective-permute-done | bytes 12320 | tf_op jit(solution)/shard_map/ppermute | solution.py:318
  42.9 0.1 join.1
  43.0 0.1 collective-permute-start.6
  43.1 1.7 %collective-permute-start.7 = (f32[2,8,768]{2,1,0:T(8,128)S(1)}, f32[2,8,768]{2,1,0:T(8,128)S(1)}, u32[]{:S(2)}, u32[]{:S(2)}) collective-permute-start(f32[2,8,768]{2,1,0:T(8,128)S(1)} %get-tuple-element.22), channel_id=1, source_target_pairs={{0,24},{8,0},{16,8},{24,16},{1,25},{9,1},{17,9},{25,17},{2,26},{10... | collective-permute-start | bytes 147464 | tf_op jit(solution)/shard_map/ppermute | solution.py:318
  44.8 1.8 %collective-permute-done.6.refs_5_ = f32[2,8,768]{2,1,0:T(8,128)S(1)} collective-permute-done((f32[2,8,768]{2,1,0:T(8,128)S(1)}, f32[2,8,768]{2,1,0:T(8,128)S(1)}, u32[]{:S(2)}, u32[]{:S(2)}) %collective-permute-start.6) | collective-permute-done | bytes 49184 | tf_op jit(solution)/shard_map/ppermute | solution.py:318
  46.6 0.0 collective-permute-done.7.refs_6_
  46.6 0.0 copy-done.1
  46.6 0.0 copy-done.2
  46.6 0.0 copy-done.3
  46.6 0.0 copy-done.4
  46.6 0.0 copy-done.5
  46.7 2.2 %filter.1 = (f32[16,16,24]{2,1,0:T(8,128)S(1)}, f32[16,384]{1,0:T(8,128)S(1)}) custom-call(f32[16,192]{1,0:T(8,128)S(1)} %copy-done.5, bf16[48,192]{1,0:T(8,128)(2,1)S(1)} %copy-done.4, bf16[48,192]{1,0:T(8,128)(2,1)S(1)} %copy-done.3, bf16[192,24]{1,0:T(8,128)(2,1)S(1)} %copy-done.2, bf16[192,24]{1,0:T(8,128)(2,1)S(1)} %copy-done.1, ...), custom_call_target="tpu_custom_call" | custom-call | tf_op jit(solution)/shard_map/filter/pallas_call | solution.py:466
  48.9 0.0 copy-start.6
  48.9 3.7 %potential.1 = (bf16[16,6,8,384]{3,2,1,0:T(8,128)(2,1)S(1)}, f32[16,16,24]{2,1,0:T(8,128)}) custom-call(s32[1,128]{1,0:T(1,128)S(1)} %get-tuple-element.17.place_vmem, f32[16,16,24]{2,1,0:T(8,128)S(1)} %get-tuple-element.24.grid_ref, f32[16,384]{1,0:T(8,128)S(1)} %get-tuple-element.25.field_ref, bf16[384,3072]{1,0:T(8,128)(2,1)S(1)} %get-tuple-element.15.near_ref, ...), custom_call_target="tpu_custom_call" | custom-call | tf_op jit(solution)/shard_map/potential/pallas_call | solution.py:481
  52.7 22.4 %all_to_all.10.back_ref = bf16[16,6,8,384]{3,2,1,0:T(8,128)(2,1)S(1)} all-to-all(bf16[16,6,8,384]{3,2,1,0:T(8,128)(2,1)S(1)} %get-tuple-element.27), channel_id=1, replica_groups=mesh['gx'=4,'gy'=4,'gz'=2] {'gx','gy'}, dimensions={0} | all-to-all | bytes 1179648 | tf_op jit(solution)/shard_map/all_to_all | solution.py:499
  75.1 0.0 copy-done.6
  75.1 1.4 %unpack.1 = bf16[48,8,384]{2,1,0:T(8,128)(2,1)} custom-call(s32[48]{0:T(128)S(1)} %copy-done.6, bf16[16,6,8,384]{3,2,1,0:T(8,128)(2,1)S(1)} %all_to_all.10.back_ref), custom_call_target="tpu_custom_call" | custom-call | tf_op jit(solution)/shard_map/unpack/pallas_call | solution.py:500
Async XLA Ops:
  2.8 25.1 %all-to-all-start = ((bf16[16,19,8,128]{3,2,1,0:T(8,128)(2,1)}), bf16[16,19,8,128]{3,2,1,0:T(8,128)(2,1)S(1)}, u32[]{:S(2)}, u32[]{:S(2)}) async-start(bf16[16,19,8,128]{3,2,1,0:T(8,128)(2,1)} %pack.1), calls=%async_computation | async-start | bytes 1245184 | tf_op jit(solution)/shard_map/all_to_all | solution.py:378
  13.3 1.4 %copy-start = (bf16[384,3072]{1,0:T(8,128)(2,1)}, bf16[384,3072]{1,0:T(8,128)(2,1)S(1)}, u32[]{:S(2)}) copy-start(bf16[384,3072]{1,0:T(8,128)(2,1)S(1)} %get-tuple-element.16.far_hbm) | copy-start | bytes 7077892
  29.8 16.8 %copy-start.1 = (bf16[192,24]{1,0:T(8,128)(2,1)S(1)}, bf16[192,24]{1,0:T(8,128)(2,1)}, u32[]{:S(2)}) copy-start(bf16[192,24]{1,0:T(8,128)(2,1)} %constant.14.clone.refs_4_) | copy-start | bytes 27652
  29.9 16.8 %copy-start.2 = (bf16[192,24]{1,0:T(8,128)(2,1)S(1)}, bf16[192,24]{1,0:T(8,128)(2,1)}, u32[]{:S(2)}) copy-start(bf16[192,24]{1,0:T(8,128)(2,1)} %constant.13.clone.refs_3_) | copy-start | bytes 27652
  29.9 16.8 %copy-start.3 = (bf16[48,192]{1,0:T(8,128)(2,1)S(1)}, bf16[48,192]{1,0:T(8,128)(2,1)}, u32[]{:S(2)}) copy-start(bf16[48,192]{1,0:T(8,128)(2,1)} %constant.12.clone.refs_2_) | copy-start | bytes 55300
  29.9 16.8 %copy-start.4 = (bf16[48,192]{1,0:T(8,128)(2,1)S(1)}, bf16[48,192]{1,0:T(8,128)(2,1)}, u32[]{:S(2)}) copy-start(bf16[48,192]{1,0:T(8,128)(2,1)} %constant.11.clone.refs_1_) | copy-start | bytes 55300
  29.9 16.8 %copy-start.5 = (f32[16,192]{1,0:T(8,128)S(1)}, f32[16,192]{1,0:T(8,128)}, u32[]{:S(2)}) copy-start(f32[16,192]{1,0:T(8,128)} %constant.10.clone.refs_0_) | copy-start | bytes 36868
  31.4 6.0 %collective-permute-start.5 = (f32[16,192]{1,0:T(8,128)S(1)}, f32[16,192]{1,0:T(8,128)S(1)}, u32[]{:S(2)}, u32[]{:S(2)}) collective-permute-start(f32[16,192]{1,0:T(8,128)S(1)} %far.1.refs_1_), channel_id=1, source_target_pairs={{0,3},{1,2},{2,1},{3,0},{4,7},{5,6},{6,5},{7,4},{8,11},{9,10},{10,... | collective-permute-start | bytes 36872 | tf_op jit(solution)/shard_map/ppermute | solution.py:318
  32.2 8.0 %collective-permute-start.3 = (f32[16,192]{1,0:T(8,128)S(1)}, f32[16,192]{1,0:T(8,128)S(1)}, u32[]{:S(2)}, u32[]{:S(2)}) collective-permute-start(f32[16,192]{1,0:T(8,128)S(1)} %far.1.refs_1_), channel_id=1, source_target_pairs={{0,1},{1,0},{2,3},{3,2},{4,5},{5,4},{6,7},{7,6},{8,9},{9,8},{10,11... | collective-permute-start | bytes 36872 | tf_op jit(solution)/shard_map/ppermute | solution.py:318
  33.0 7.2 %collective-permute-start.1 = (f32[16,192]{1,0:T(8,128)S(1)}, f32[16,192]{1,0:T(8,128)S(1)}, u32[]{:S(2)}, u32[]{:S(2)}) collective-permute-start(f32[16,192]{1,0:T(8,128)S(1)} %far.1.refs_1_), channel_id=1, source_target_pairs={{0,2},{2,0},{4,6},{6,4},{1,3},{3,1},{5,7},{7,5},{8,10},{10,8},{12,... | collective-permute-start | bytes 36872 | tf_op jit(solution)/shard_map/ppermute | solution.py:318
  34.9 6.4 %collective-permute-start.4 = (f32[16,192]{1,0:T(8,128)S(1)}, f32[16,192]{1,0:T(8,128)S(1)}, u32[]{:S(2)}, u32[]{:S(2)}) collective-permute-start(f32[16,192]{1,0:T(8,128)S(1)} %get-tuple-element.18.refs_0_), channel_id=1, source_target_pairs={{0,7},{1,6},{2,5},{3,4},{4,3},{5,2},{6,1},{7,0},{8,15},{9,14},{10,... | collective-permute-start | bytes 36872 | tf_op jit(solution)/shard_map/ppermute | solution.py:318
  36.9 4.5 %collective-permute-start.2 = (f32[16,192]{1,0:T(8,128)S(1)}, f32[16,192]{1,0:T(8,128)S(1)}, u32[]{:S(2)}, u32[]{:S(2)}) collective-permute-start(f32[16,192]{1,0:T(8,128)S(1)} %get-tuple-element.18.refs_0_), channel_id=1, source_target_pairs={{0,1},{1,0},{2,3},{3,2},{4,5},{5,4},{6,7},{7,6},{8,9},{9,8},{10,11... | collective-permute-start | bytes 36872 | tf_op jit(solution)/shard_map/ppermute | solution.py:318
  37.4 5.5 %collective-permute-start = (f32[16,192]{1,0:T(8,128)S(1)}, f32[16,192]{1,0:T(8,128)S(1)}, u32[]{:S(2)}, u32[]{:S(2)}) collective-permute-start(f32[16,192]{1,0:T(8,128)S(1)} %get-tuple-element.18.refs_0_), channel_id=1, source_target_pairs={{0,6},{2,4},{4,2},{6,0},{1,7},{3,5},{5,3},{7,1},{8,14},{10,12},{12... | collective-permute-start | bytes 36872 | tf_op jit(solution)/shard_map/ppermute | solution.py:318
  43.0 3.6 %collective-permute-start.6 = (f32[2,8,768]{2,1,0:T(8,128)S(1)}, f32[2,8,768]{2,1,0:T(8,128)S(1)}, u32[]{:S(2)}, u32[]{:S(2)}) collective-permute-start(f32[2,8,768]{2,1,0:T(8,128)S(1)} %get-tuple-element.21), channel_id=1, source_target_pairs={{0,8},{8,16},{16,24},{24,0},{1,9},{9,17},{17,25},{25,1},{2,10},{10... | collective-permute-start | bytes 147464 | tf_op jit(solution)/shard_map/ppermute | solution.py:318
  43.1 3.5 %collective-permute-start.7 = (f32[2,8,768]{2,1,0:T(8,128)S(1)}, f32[2,8,768]{2,1,0:T(8,128)S(1)}, u32[]{:S(2)}, u32[]{:S(2)}) collective-permute-start(f32[2,8,768]{2,1,0:T(8,128)S(1)} %get-tuple-element.22), channel_id=1, source_target_pairs={{0,24},{8,0},{16,8},{24,16},{1,25},{9,1},{17,9},{25,17},{2,26},{10... | collective-permute-start | bytes 147464 | tf_op jit(solution)/shard_map/ppermute | solution.py:318
  48.9 26.2 %copy-start.6 = (s32[48]{0:T(128)S(1)}, s32[48]{0:T(128)}, u32[]{:S(2)}) copy-start(s32[48]{0:T(128)} %tile_ref.1) | copy-start | bytes 580
